TPU v7x, 32 devices: a whole 2x2x4 slice. The times are simulated.
32 devices in a mesh: tower: 2 (over core), batch: 16 (over z, y, x).
Axes of the slice: x: 2, y: 2, z: 4, core: 2. Of those that a mesh axis runs over, the one named last changes fastest.
Arguments:
- tokens: bfloat16 [2, 32768, 768], P('tower', 'batch'), may hold values from -6 to 6
- lengths: int32 [2, 64], P('tower', 'batch'), may hold values from 64 to 512, as said below
- prefixes: int32 [2, 64], P('tower', 'batch'), may hold values from 1 to 32
- positives: int32 [64], replicated, may hold values from 0 to 63, each once
- gain_attention: float32 [768], replicated, may hold values from 0.5 to 1.5
- query_weight: bfloat16 [768, 768], replicated, may hold values from -0.02734375 to 0.02734375
- key_weight: bfloat16 [768, 768], replicated, may hold values from -0.21875 to 0.21875
- value_weight: bfloat16 [768, 768], replicated, may hold values from -0.21875 to 0.21875
- output_weight: bfloat16 [768, 768], replicated, may hold values from -1.75 to 1.75
- bucket_bias: float32 [32, 12], replicated, may hold values from -4 to 4
- gain_feedforward: float32 [768], replicated, may hold values from 0.5 to 1.5
- widen_weight: bfloat16 [768, 3072], replicated, may hold values from -0.21875 to 0.21875
- narrow_weight: bfloat16 [3072, 768], replicated, may hold values from -0.109375 to 0.109375
- gain_final: float32 [768], replicated, may hold values from 0.5 to 1.5
Outputs:
- contrast_loss: float32 [], replicated
- score_gradient: float32 [64, 64], P('batch')
- token_gradient: bfloat16 [2, 32768, 768], P('tower', 'batch')
- grad_attention: float32 [768], replicated
- grad_query: float32 [768, 768], replicated
- grad_key: float32 [768, 768], replicated
- grad_value: float32 [768, 768], replicated
- grad_output: float32 [768, 768], replicated
- grad_bucket: float32 [32, 12], replicated
- grad_feedforward: float32 [768], replicated
- grad_widen: float32 [768, 3072], replicated
- grad_narrow: float32 [3072, 768], replicated
- grad_final: float32 [768], replicated
Inputs may be any that keep to these rules, and one draw needn't show every extreme that they name: `lengths`: sequence 0 of each side uses all 512 positions. `positives`: every document is the positive of exactly one query.
All inputs are finite; a program needn't handle non-finite values.
Results may differ from a plain program's by a relative error of at most 0.025.
The roundings to bfloat16 on the way count: a program that leaves them out, or rounds other values in their place, can miss the bound.
Values sent between devices are 32-bit elements; how exact they have to be, the bound alone decides.
A program may use at most 320 MiB of HBM per device.

v0:
```python
import jax
import jax.numpy as jnp
from jax import lax
from jax.sharding import PartitionSpec as P

epsilon = 1e-06
masked_score = -1000000000.0
score_scale = 100.0
far_steps = (12, 16, 23, 32, 46, 64, 91)
highest = lax.Precision.HIGHEST


def bucket_onehot(slot_len, bucket_count):
    places = jnp.arange(slot_len, dtype=jnp.int32)
    offset = places[None, :] - places[:, None]
    spread = jnp.abs(offset)
    far_bucket = 8 + sum(((spread >= step).astype(jnp.int32) for step in far_steps))
    bucket = jnp.where(spread < 8, spread, far_bucket) + jnp.where(
        offset > 0, bucket_count // 2, 0
    ).astype(jnp.int32)
    labels = jnp.arange(bucket_count, dtype=jnp.int32)
    return (bucket[:, :, None] == labels[None, None, :]).astype(jnp.float32)


def norm_forward(values, scale_vec):
    inverse = lax.rsqrt(jnp.mean(values * values, axis=-1, keepdims=True) + epsilon)
    return (values * inverse * scale_vec, inverse)


def norm_backward(values, inverse, scale_vec, upstream):
    scaled = upstream * scale_vec
    inner_mean = jnp.mean(scaled * values, axis=-1, keepdims=True)
    grad_values = inverse * scaled - values * (inverse * inverse * inverse) * inner_mean
    grad_scale = jnp.sum(upstream * values * inverse, axis=0)
    return (grad_values, grad_scale)


def local(
    tokens,
    lengths,
    prefixes,
    positives,
    gain_attention,
    query_weight,
    key_weight,
    value_weight,
    output_weight,
    bucket_bias,
    gain_feedforward,
    widen_weight,
    narrow_weight,
    gain_final,
):
    seqs = lengths.shape[1]
    rows = tokens.shape[1]
    slot_len = rows // seqs
    width = tokens.shape[2]
    heads = bucket_bias.shape[1]
    head_dim = query_weight.shape[1] // heads
    inner = heads * head_dim
    tokens_f = tokens[0].astype(jnp.float32)
    seq_lengths = lengths[0]
    seq_prefix = prefixes[0]
    onehot = bucket_onehot(slot_len, bucket_bias.shape[0])
    bias = jnp.einsum("ijb,bh->hij", onehot, bucket_bias, precision=highest)
    normed_f, inverse_first = norm_forward(tokens_f, gain_attention)
    normed = normed_f.astype(jnp.bfloat16)

    def project(matrix):
        projected = jnp.dot(normed, matrix, preferred_element_type=jnp.float32).astype(jnp.bfloat16)
        return projected.reshape(seqs, slot_len, heads, head_dim)

    query_all = project(query_weight)
    key_all = project(key_weight)
    value_all = project(value_weight)
    places = jnp.arange(slot_len, dtype=jnp.int32)
    valid = places[None, :] < seq_lengths[:, None]

    def score_block(query_rows, key_rows, valid_keys):
        raw_scores = jnp.einsum(
            "ihd,jhd->hij", query_rows, key_rows, preferred_element_type=jnp.float32
        )
        return jnp.where(valid_keys[None, None, :], raw_scores + bias, masked_score)

    def attend_forward(parts):
        query_rows, key_rows, value_rows, valid_keys = parts
        scores = score_block(query_rows, key_rows, valid_keys)
        row_peak = jnp.max(scores, axis=-1, keepdims=True)
        raised = jnp.exp(scores - row_peak)
        totals = jnp.sum(raised, axis=-1, keepdims=True)
        soft_low = (raised / totals).astype(jnp.bfloat16)
        context = jnp.einsum(
            "hij,jhd->ihd", soft_low, value_rows, preferred_element_type=jnp.float32
        )
        return (context.astype(jnp.bfloat16), (row_peak + jnp.log(totals))[:, :, 0])

    context, log_totals = lax.map(attend_forward, (query_all, key_all, value_all, valid))
    context_flat = context.reshape(rows, inner)
    mixed = tokens_f + jnp.dot(context_flat, output_weight, preferred_element_type=jnp.float32)
    ffn_in_f, inverse_second = norm_forward(mixed, gain_feedforward)
    ffn_in = ffn_in_f.astype(jnp.bfloat16)
    pre_act = jnp.dot(ffn_in, widen_weight, preferred_element_type=jnp.float32)
    hidden = jnp.where(pre_act > 0, pre_act, 0.0).astype(jnp.bfloat16)
    output = mixed + jnp.dot(hidden, narrow_weight, preferred_element_type=jnp.float32)
    final, inverse_third = norm_forward(output, gain_final)
    pool_mask = ((places[None, :] >= seq_prefix[:, None]) & valid).astype(jnp.float32)
    pool_weight = pool_mask / jnp.sum(pool_mask, axis=1, keepdims=True)
    pooled = jnp.sum(final.reshape(seqs, slot_len, width) * pool_weight[:, :, None], axis=1)
    inverse_pool = lax.rsqrt(jnp.sum(pooled * pooled, axis=-1, keepdims=True) + epsilon)
    unit = pooled * inverse_pool
    gathered = lax.all_gather(unit, ("tower", "batch"), axis=0, tiled=True)
    total_seqs = gathered.shape[0] // 2
    query_units = gathered[:total_seqs]
    doc_units = gathered[total_seqs:]
    scores = score_scale * jnp.dot(query_units, doc_units.T, precision=highest)
    labels = jnp.arange(total_seqs, dtype=jnp.int32)
    target = (positives[:, None] == labels[None, :]).astype(jnp.float32)
    row_peak = jnp.max(scores, axis=1, keepdims=True)
    row_raised = jnp.exp(scores - row_peak)
    row_sum = jnp.sum(row_raised, axis=1, keepdims=True)
    col_peak = jnp.max(scores, axis=0, keepdims=True)
    col_raised = jnp.exp(scores - col_peak)
    col_sum = jnp.sum(col_raised, axis=0, keepdims=True)
    loss_value = (
        0.5 * jnp.sum(row_peak[:, 0] + jnp.log(row_sum[:, 0]))
        + 0.5 * jnp.sum(col_peak[0] + jnp.log(col_sum[0]))
        - jnp.sum(target * scores)
    )
    score_grad = 0.5 * row_raised / row_sum + 0.5 * col_raised / col_sum - target
    tower = lax.axis_index("tower")
    first_row = lax.axis_index("batch") * seqs
    my_rows = lax.dynamic_slice_in_dim(score_grad, first_row, seqs, 0)
    my_cols = lax.dynamic_slice_in_dim(score_grad, first_row, seqs, 1)
    grad_as_query = score_scale * jnp.dot(my_rows, doc_units, precision=highest)
    grad_as_doc = score_scale * jnp.dot(my_cols.T, query_units, precision=highest)
    grad_unit = jnp.where(tower == 0, grad_as_query, grad_as_doc)
    cubed = inverse_pool * inverse_pool * inverse_pool
    grad_pooled = inverse_pool * grad_unit - pooled * cubed * jnp.sum(
        grad_unit * pooled, axis=-1, keepdims=True
    )
    grad_fin = (pool_weight[:, :, None] * grad_pooled[:, None, :]).reshape(rows, width)
    grad_out, grad_final = norm_backward(output, inverse_third, gain_final, grad_fin)
    grad_branch = grad_out.astype(jnp.bfloat16)
    grad_narrow = jnp.einsum("tf,td->fd", hidden, grad_branch, preferred_element_type=jnp.float32)
    grad_hidden = jnp.einsum(
        "td,fd->tf", grad_branch, narrow_weight, preferred_element_type=jnp.float32
    )
    grad_pre = jnp.where(pre_act > 0, grad_hidden, 0.0).astype(jnp.bfloat16)
    grad_widen = jnp.einsum("td,tf->df", ffn_in, grad_pre, preferred_element_type=jnp.float32)
    grad_ffn_in = jnp.einsum(
        "tf,df->td", grad_pre, widen_weight, preferred_element_type=jnp.float32
    )
    grad_mixed_norm, grad_feedforward = norm_backward(
        mixed, inverse_second, gain_feedforward, grad_ffn_in
    )
    grad_mixed = grad_out + grad_mixed_norm
    grad_attn = grad_mixed.astype(jnp.bfloat16)
    grad_output = jnp.einsum(
        "ti,td->id", context_flat, grad_attn, preferred_element_type=jnp.float32
    )
    grad_context = jnp.einsum(
        "td,id->ti", grad_attn, output_weight, preferred_element_type=jnp.float32
    )
    grad_context = grad_context.astype(jnp.bfloat16).reshape(seqs, slot_len, heads, head_dim)

    def attend_backward(bias_total, parts):
        query_rows, key_rows, value_rows, valid_keys, log_rows, context_grad = parts
        scores_here = score_block(query_rows, key_rows, valid_keys)
        soft = jnp.exp(scores_here - log_rows[:, :, None])
        soft_low = soft.astype(jnp.bfloat16)
        value_part = jnp.einsum(
            "hij,ihd->jhd", soft_low, context_grad, preferred_element_type=jnp.float32
        )
        grad_soft = jnp.einsum(
            "ihd,jhd->hij", context_grad, value_rows, preferred_element_type=jnp.float32
        )
        grad_scores = soft * (grad_soft - jnp.sum(grad_soft * soft, axis=-1, keepdims=True))
        scores_low = grad_scores.astype(jnp.bfloat16)
        query_part = jnp.einsum(
            "hij,jhd->ihd", scores_low, key_rows, preferred_element_type=jnp.float32
        )
        key_part = jnp.einsum(
            "hij,ihd->jhd", scores_low, query_rows, preferred_element_type=jnp.float32
        )
        return (
            bias_total + grad_scores,
            (
                query_part.astype(jnp.bfloat16),
                key_part.astype(jnp.bfloat16),
                value_part.astype(jnp.bfloat16),
            ),
        )

    bias_total, (query_grads, key_grads, value_grads) = lax.scan(
        attend_backward,
        jnp.zeros(bias.shape, jnp.float32),
        (query_all, key_all, value_all, valid, log_totals, grad_context),
    )
    query_grads = query_grads.reshape(rows, inner)
    key_grads = key_grads.reshape(rows, inner)
    value_grads = value_grads.reshape(rows, inner)
    grad_bucket = jnp.einsum("ijb,hij->bh", onehot, bias_total, precision=highest)
    grad_query = jnp.einsum("td,ti->di", normed, query_grads, preferred_element_type=jnp.float32)
    grad_key = jnp.einsum("td,ti->di", normed, key_grads, preferred_element_type=jnp.float32)
    grad_value = jnp.einsum("td,ti->di", normed, value_grads, preferred_element_type=jnp.float32)
    grad_normed = (
        jnp.einsum("ti,di->td", query_grads, query_weight, preferred_element_type=jnp.float32)
        + jnp.einsum("ti,di->td", key_grads, key_weight, preferred_element_type=jnp.float32)
        + jnp.einsum("ti,di->td", value_grads, value_weight, preferred_element_type=jnp.float32)
    )
    grad_tokens_norm, grad_attention = norm_backward(
        tokens_f, inverse_first, gain_attention, grad_normed
    )
    token_gradient = (grad_mixed + grad_tokens_norm).astype(jnp.bfloat16)[None]
    (
        sum_attention,
        sum_query,
        sum_key,
        sum_value,
        sum_output,
        sum_bucket,
        sum_feedforward,
        sum_widen,
        sum_narrow,
        sum_final,
    ) = lax.psum(
        (
            grad_attention,
            grad_query,
            grad_key,
            grad_value,
            grad_output,
            grad_bucket,
            grad_feedforward,
            grad_widen,
            grad_narrow,
            grad_final,
        ),
        ("tower", "batch"),
    )
    return (
        loss_value,
        my_rows,
        token_gradient,
        sum_attention,
        sum_query,
        sum_key,
        sum_value,
        sum_output,
        sum_bucket,
        sum_feedforward,
        sum_widen,
        sum_narrow,
        sum_final,
    )


def solution(mesh):
    placed = (
        P("tower", "batch", None),
        P("tower", "batch"),
        P("tower", "batch"),
        P(),
        P(),
        P(),
        P(),
        P(),
        P(),
        P(),
        P(),
        P(),
        P(),
        P(),
    )
    return jax.shard_map(
        local,
        mesh=mesh,
        in_specs=placed,
        out_specs=(
            P(),
            P("batch", None),
            P("tower", "batch", None),
            P(),
            P(),
            P(),
            P(),
            P(),
            P(),
            P(),
            P(),
            P(),
            P(),
        ),
        check_vma=False,
    )
```

profile of v0, /device:TPU:0, one launch (start us, length us, event | category | flops | bytes accessed | tf_op | source)
XLA Modules:
  0.0 1078.6 jit_solution(5208512605683882147)
XLA Ops:
  74.6 13.7 %fusion.55 = f32[12,512,512]{2,0,1:T(8,128)} fusion(s32[512,512]{1,0:T(8,128)S(1)} %fusion.93, f32[32,12]{0,1:T(8,128)S(1)} %copy-done.36), kind=kOutput, calls=%fused_computation.65 | convolution fusion | flops 1216348160 | bytes 13633024 | tf_op jit(solution)/shard_map/ijb,bh->hij/dot_general | solution.py:65
  88.2 17.3 %copy.73 = f32[12,512,512]{1,2,0:T(8,128)} copy(f32[12,512,512]{2,0,1:T(8,128)} %fusion.55) | data formatting | bytes 25165824 | tf_op jit(solution)/shard_map/while | solution.py:97
  107.6 59.8 %while.29 = (s32[]{:T(128)}, bf16[4,512,12,64]{1,3,2,0:T(8,128)(2,1)}, f32[4,12,512]{2,1,0:T(8,128)}, bf16[4,512,12,64]{1,3,2,0:T(8,128)(2,1)}, pred[4,512]{1,0:...) while((s32[]{:T(128)}, ...), condition=%wide.region_4.5_spmd, body=%wide.region_1.4_spmd.sunk | while | flops 830859264 | bytes 53685868 | solution.py:97
  179.0 13.7 %fusion.113 = f32[2048,3072]{1,0:T(8,128)} fusion(bf16[768,3072]{1,0:T(8,128)(2,1)S(1)} %bitcast.270, f32[2048,768]{1,0:T(8,128)S(1)} %get-tuple-element.306, f32[768]{0:T(1024)S(1)} %copy-done.46, f32[2048]{0:T(1024)S(1)} %get-tuple-element.298), kind=kOutput, calls=%fused_computation.170 | convolution fusion | flops 9668395008 | bytes 36187136 | tf_op jit(solution)/shard_map/dot_general | solution.py:102
  192.7 19.2 %multiply_reduce_fusion.4 = (f32[2048]{0:T(1024)S(1)}, f32[2048,768]{1,0:T(8,128)}) fusion(f32[2048,768]{1,0:T(8,128)} %copy-done.16, bf16[3072,768]{1,0:T(8,128)(2,1)} %param.30, f32[2048,3072]{1,0:T(8,128)} %fusion.113), kind=kOutput, calls=%fused_computation.101 | convolution fusion | flops 9687267328 | bytes 42475520 | tf_op jit(solution)/shard_map/dot_general | solution.py:104
  215.5 72.1 %all-gather = f32[32,4,768]{2,1,0:T(4,128)S(1)} all-gather(f32[1,4,768]{2,1,0:T(4,128)S(1)} %multiply_bitcast_fusion), channel_id=1, replica_groups=mesh['tower'=2,'batch'=16] {'tower','batch'}, dimensions={0}, use_global_device_ids=true | all-gather | bytes 405504 | tf_op jit(solution)/shard_map/all_gather | solution.py:111
  300.3 18.3 %fusion.83 = f32[3072,768]{1,0:T(8,128)} fusion(bf16[2048,768]{1,0:T(8,128)(2,1)} %fusion.82, f32[2048,3072]{1,0:T(8,128)} %fusion.113), kind=kOutput, calls=%fused_computation.110 | convolution fusion | flops 9682550784 | bytes 37748736 | tf_op jit(solution)/shard_map/tf,td->fd/dot_general | solution.py:144
  318.5 20.8 %fusion.52 = bf16[2048,3072]{1,0:T(8,128)(2,1)} fusion(f32[2048,3072]{1,0:T(8,128)} %fusion.113, bf16[2048,768]{1,0:T(8,128)(2,1)} %fusion.82, bf16[3072,768]{1,0:T(8,128)(2,1)} %param.30), kind=kOutput, calls=%fused_computation.62 | convolution fusion | flops 9682550784 | bytes 45613056 | tf_op jit(solution)/shard_map/td,fd->tf/dot_general | solution.py:145
  339.4 17.4 %multiply_reduce_fusion.1 = (f32[768]{0:T(1024)}, f32[2048]{0:T(1024)S(1)}, f32[2048,768]{1,0:T(8,128)}) fusion(f32[2048,768]{1,0:T(8,128)S(1)} %bitcast.254, f32[2048]{0:T(1024)S(1)} %get-tuple-element.298, f32[768]{0:T(1024)S(1)} %copy-done.46, bf16[2048,3072]{1,0:T(8,128)(2,1)} %fusion.52, bf16[768,3072]{1,0:T(8,128)(2,1)} %param.29), kind=kOutput, calls=%fused_computation.95 | convolution fusion | flops 9673110528 | bytes 29906944 | tf_op jit(solution)/shard_map/tf,df->td/dot_general | solution.py:150
  356.8 15.6 %fusion.112 = f32[768,3072]{1,0:T(8,128)} fusion(bf16[2048,3072]{1,0:T(8,128)(2,1)} %fusion.52, f32[2048,768]{1,0:T(8,128)S(1)} %bitcast.254, f32[768]{0:T(1024)S(1)} %copy-done.46, f32[2048]{0:T(1024)S(1)} %get-tuple-element.298), kind=kOutput, calls=%fused_computation.169 | convolution fusion | flops 9668395008 | bytes 28322816 | tf_op jit(solution)/shard_map/td,tf->df/dot_general | solution.py:149
  405.7 183.0 %while.30 = (s32[]{:T(128)}, f32[12,512,512]{1,2,0:T(8,128)}, bf16[4,512,12,64]{1,3,2,0:T(8,128)(2,1)}, bf16[4,512,12,64]{1,3,2,0:T(8,128)(2,1)}, bf16[4,512,12,...) while((s32[]{:T(128)}, f32[12,512,512]{1,2,0:T(8,128)}, ...), condition=%wide.region_22.23_spmd.clone, body=%wide.region_20.22_spmd.clone.sunk | while | flops 2049042432 | bytes 177863392 | solution.py:194
  406.5 8.8 subtract_exponential_fusion.5
  425.8 13.5 %fusion.188 = (bf16[12,512,512]{1,2,0:T(8,128)(2,1)}, f32[12,512,512]{1,2,0:T(8,128)}) fusion(f32[12,512,512]{1,2,0:T(8,128)S(1)} %subtract_exponential_fusion.5, f32[12,512,512]{1,2,0:T(8,128)} %get-tuple-element.446, f32[12,512]{1,0:T(8,128)S(1)} %get-tuple-element.447, f32[12,512,512]{1,2,0:T(8,128)} %get-tuple-element.492, pred[]{:T(512)S(6)} %compare.3), kind=kLoop, calls=%fused_computation.24.clone.1 | loop fusion | flops 15728640 | bytes 56647680 | tf_op jit(solution)/shard_map/while/body/eval_jaxpr/convert_element_type | solution.py:178
  449.3 8.8 subtract_exponential_fusion.5
  468.6 17.4 %fusion.188 = (bf16[12,512,512]{1,2,0:T(8,128)(2,1)}, f32[12,512,512]{1,2,0:T(8,128)}) fusion(f32[12,512,512]{1,2,0:T(8,128)S(1)} %subtract_exponential_fusion.5, f32[12,512,512]{1,2,0:T(8,128)} %get-tuple-element.446, f32[12,512]{1,0:T(8,128)S(1)} %get-tuple-element.447, f32[12,512,512]{1,2,0:T(8,128)} %get-tuple-element.492, pred[]{:T(512)S(6)} %compare.3), kind=kLoop, calls=%fused_computation.24.clone.1 | loop fusion | flops 15728640 | bytes 56647680 | tf_op jit(solution)/shard_map/while/body/eval_jaxpr/convert_element_type | solution.py:178
  515.3 17.4 %fusion.188 = (bf16[12,512,512]{1,2,0:T(8,128)(2,1)}, f32[12,512,512]{1,2,0:T(8,128)}) fusion(f32[12,512,512]{1,2,0:T(8,128)S(1)} %subtract_exponential_fusion.5, f32[12,512,512]{1,2,0:T(8,128)} %get-tuple-element.446, f32[12,512]{1,0:T(8,128)S(1)} %get-tuple-element.447, f32[12,512,512]{1,2,0:T(8,128)} %get-tuple-element.492, pred[]{:T(512)S(6)} %compare.3), kind=kLoop, calls=%fused_computation.24.clone.1 | loop fusion | flops 15728640 | bytes 56647680 | tf_op jit(solution)/shard_map/while/body/eval_jaxpr/convert_element_type | solution.py:178
  542.6 8.8 subtract_exponential_fusion.5
  561.9 17.4 %fusion.188 = (bf16[12,512,512]{1,2,0:T(8,128)(2,1)}, f32[12,512,512]{1,2,0:T(8,128)}) fusion(f32[12,512,512]{1,2,0:T(8,128)S(1)} %subtract_exponential_fusion.5, f32[12,512,512]{1,2,0:T(8,128)} %get-tuple-element.446, f32[12,512]{1,0:T(8,128)S(1)} %get-tuple-element.447, f32[12,512,512]{1,2,0:T(8,128)} %get-tuple-element.492, pred[]{:T(512)S(6)} %compare.3), kind=kLoop, calls=%fused_computation.24.clone.1 | loop fusion | flops 15728640 | bytes 56647680 | tf_op jit(solution)/shard_map/while/body/eval_jaxpr/convert_element_type | solution.py:178
  617.3 18.7 %copy.84 = f32[12,512,512]{2,0,1:T(8,128)} copy(f32[12,512,512]{1,2,0:T(8,128)} %get-tuple-element.126) | data formatting | bytes 25165824 | tf_op jit(solution)/shard_map/while | solution.py:194
  654.5 17.5 %fusion.92 = f32[32,12]{0,1:T(8,128)S(1)} fusion(f32[12,512,512]{2,0,1:T(8,128)S(1)} %copy-done.2, s32[512,512]{1,0:T(8,128)S(1)} %copy-done.11), kind=kOutput, calls=%fused_computation.121 | convolution fusion | flops 1216348160 | bytes 13633024 | tf_op jit(solution)/shard_map/ijb,hij->bh/dot_general | solution.py:202
  672.1 9.1 fusion.71
  681.2 39.6 %all-reduce = (f32[768]{0:T(1024)}, f32[32,12]{0,1:T(8,128)}, f32[768]{0:T(1024)}, f32[768]{0:T(1024)}) all-reduce(f32[768]{0:T(1024)S(1)} %get-tuple-element.228, f32[32,12]{0,1:T(8,128)S(1)} %fusion.92, f32[768]{0:T(1024)S(1)} %copy-done.47, f32[768]{0:T(1024)S(1)} %copy-done.33), channel_id=1, replica_groups=mesh['tower'=2,'batch'=16] {'tower','batch'}, use_global_device_ids=true, to_apply=%region_25.26 | all-reduce | flops 2688 | bytes 21504 | tf_op jit(solution)/shard_map/psum | solution.py:226
  729.1 320.5 %all-reduce.4.cloned.1.call-done = (f32[768,768]{1,0:T(8,128)}, f32[768,768]{1,0:T(8,128)}, f32[768,768]{1,0:T(8,128)}, f32[768,768]{1,0:T(8,128)}, f32[768,3072]{1,0:T(8,128)}, /*index=5*/f32[3072,768]{1,0:T(8,128)}) async-done(((f32[768,768]{1,0:T(8,128)}, f32[768,768]{1,0:T(8,128)}, f32[768,768]{1,0:T(8,128)}, f32[768,768]{1,0:T(8,128)}, f32[768,3072]{1,0:T(8,128)}, /*index=5*/f32[3072,768]{1,0:T(8,128)}), ...) | async-done | bytes 28311568 | tf_op jit(solution)/shard_map/psum | solution.py:226
  1057.3 9.3 copy.133
  (260 shorter events, 344.7 us)
Async XLA Ops:
  7.2 48.2 %copy-start = (bf16[768,768]{1,0:T(8,128)(2,1)S(1)}, bf16[768,768]{1,0:T(8,128)(2,1)}, u32[]{:S(2)}) copy-start(bf16[768,768]{1,0:T(8,128)(2,1)} %param.25) | copy-start | bytes 3538948
  7.2 1042.5 %all-reduce.4.cloned.1.call-start = ((), (), s32[]{:S(2)}) async-start(), calls=%async_computation | async-start | bytes 56623104 | tf_op jit(solution)/shard_map/psum | solution.py:226
  7.7 66.9 %copy-start.10 = (s32[512,512]{1,0:T(8,128)}, s32[512,512]{1,0:T(8,128)S(1)}, u32[]{:S(2)}) copy-start(s32[512,512]{1,0:T(8,128)S(1)} %fusion.93) | copy-start | bytes 3145732
  12.5 42.9 %copy-start.27 = (f32[2048]{0:T(1024)}, f32[2048]{0:T(1024)S(1)}, u32[]{:S(2)}) copy-start(f32[2048]{0:T(1024)S(1)} %get-tuple-element.296) | copy-start | bytes 24580
  25.4 10.7 copy-start.52
  192.7 19.2 %copy-start.29 = (f32[768]{0:T(1024)S(1)}, f32[768]{0:T(1024)}, u32[]{:S(2)}) copy-start(f32[768]{0:T(1024)} %param.31) | copy-start | bytes 9220
  192.7 19.2 %copy-start.31 = (f32[4,512]{1,0:T(4,128)S(1)}, f32[4,512]{1,0:T(4,128)}, u32[]{:S(2)}) copy-start(f32[4,512]{1,0:T(4,128)} %get-tuple-element.302) | copy-start | bytes 24580
  211.9 76.4 %copy-start.48 = (s32[64]{0:T(128)S(1)}, s32[64]{0:T(128)}, u32[]{:S(2)}) copy-start(s32[64]{0:T(128)} %param.21) | copy-start | bytes 772
  211.9 78.2 %copy-start.32 = (f32[1,4,4,128]{3,2,1,0:T(4,128)S(1)}, f32[1,4,4,128]{3,2,1,0:T(4,128)}, u32[]{:S(2)}) copy-start(f32[1,4,4,128]{3,2,1,0:T(4,128)} %get-tuple-element.301) | copy-start | bytes 24580
  295.3 44.0 %slice-start.5 = ((s8[6291456]{0:T(1024)(128)(4,1)}), s8[4194304]{0:T(1024)(128)(4,1)S(1)}, s32[]{:S(2)}) async-start(s8[6291456]{0:T(1024)(128)(4,1)} %bitcast.253), calls=%async_computation.6 | async-start | bytes 8388608
  300.3 39.1 %slice-start.6 = ((s8[6291456]{0:T(1024)(128)(4,1)}), s8[2097152]{0:T(1024)(128)(4,1)S(1)}, s32[]{:S(2)}) async-start(s8[6291456]{0:T(1024)(128)(4,1)} %bitcast.253), calls=%async_computation.7 | async-start | bytes 4194304
  318.5 53.8 %slice-start = ((s8[6291456]{0:T(1024)(128)(4,1)}), s8[2097152]{0:T(1024)(128)(4,1)S(1)}, s32[]{:S(2)}) async-start(s8[6291456]{0:T(1024)(128)(4,1)} %bitcast.243), calls=%async_computation.1 | async-start | bytes 4194304
  339.4 33.0 %slice-start.1 = ((s8[6291456]{0:T(1024)(128)(4,1)}), s8[4194304]{0:T(1024)(128)(4,1)S(1)}, s32[]{:S(2)}) async-start(s8[6291456]{0:T(1024)(128)(4,1)} %bitcast.243), calls=%async_computation.2 | async-start | bytes 8388608
  356.8 15.6 %copy-start.17 = (f32[2048,768]{1,0:T(8,128)S(1)}, f32[2048,768]{1,0:T(8,128)}, u32[]{:S(2)}) copy-start(f32[2048,768]{1,0:T(8,128)} %get-tuple-element.312) | copy-start | bytes 18874372
  617.2 18.7 %copy-start.38 = (f32[64]{0:T(128)S(1)}, f32[64]{0:T(128)}, u32[]{:S(2)}) copy-start(f32[64]{0:T(128)} %copy-done.37) | copy-start | bytes 772
  617.2 18.7 %copy-start.40 = (f32[64]{0:T(128)S(1)}, f32[64]{0:T(128)}, u32[]{:S(2)}) copy-start(f32[64]{0:T(128)} %copy-done.39) | copy-start | bytes 772
  617.3 18.7 %copy-start.43 = (f32[64]{0:T(128)S(1)}, f32[64]{0:T(128)}, u32[]{:S(2)}) copy-start(f32[64]{0:T(128)} %copy-done.42) | copy-start | bytes 772
  617.3 18.7 %copy-start.45 = (f32[64]{0:T(128)S(1)}, f32[64]{0:T(128)}, u32[]{:S(2)}) copy-start(f32[64]{0:T(128)} %copy-done.44) | copy-start | bytes 772
  617.3 21.3 %copy-start.51 = (bf16[768,768]{1,0:T(8,128)(2,1)S(1)}, bf16[768,768]{1,0:T(8,128)(2,1)}, u32[]{:S(2)}) copy-start(bf16[768,768]{1,0:T(8,128)(2,1)} %param.23) | copy-start | bytes 3538948
  638.5 16.0 %copy-start.2 = (f32[12,512,512]{2,0,1:T(8,128)S(1)}, f32[12,512,512]{2,0,1:T(8,128)}, u32[]{:S(2)}) copy-start(f32[12,512,512]{2,0,1:T(8,128)} %copy.84) | copy-start | bytes 37748740
  654.5 17.5 %copy-start.8 = (bf16[1,2048,768]{2,1,0:T(8,128)(2,1)S(1)}, bf16[1,2048,768]{2,1,0:T(8,128)(2,1)}, u32[]{:S(2)}) copy-start(bf16[1,2048,768]{2,1,0:T(8,128)(2,1)} %param.18) | copy-start | bytes 9437188
  654.5 17.5 %copy-start.15 = (bf16[96,8,4,512]{3,1,2,0:T(8,128)(2,1)S(1)}, bf16[96,8,4,512]{3,1,2,0:T(8,128)(2,1)}, u32[]{:S(2)}) copy-start(bf16[96,8,4,512]{3,1,2,0:T(8,128)(2,1)} %copy-done.14) | copy-start | bytes 9437188
  672.1 48.7 %copy-start.30 = (f32[2048]{0:T(1024)S(1)}, f32[2048]{0:T(1024)}, u32[]{:S(2)}) copy-start(f32[2048]{0:T(1024)} %get-tuple-element.295) | copy-start | bytes 24580
  1055.9 10.7 slice-start.2
  (45 other events, 266.8 us)
Sparse Core Ops, SparseCore 0:
  617.4 432.2 all-reduce.3
where the time goes:
time: 1080 us
  matrix products  366 us (34%)
  waiting for transfers between devices  321 us (30%)
  local copies, waits for them, and re-layouts  153 us (14%)
  blocking collectives  112 us (10%)
  other arithmetic  109 us (10%)
  between operations  18 us (2%)
    psum x1, waiting for transfers between devices, local(): lax.psum((grad_attention, grad_query, grad_key, grad_value, grad_output,...  321 us
    all_gather x1, blocking collectives, local(): gathered = lax.all_gather(unit, ('tower', 'batch'), axis=0, tiled=True)  72.1 us
    dot_general x8, matrix products, score_block(): jnp.einsum('ihd,jhd->hij', query_rows, key_rows, preferred_element_type=j...  67.1 us
    convert_element_type x4, other arithmetic, attend_backward(): scores_low = grad_scores.astype(jnp.bfloat16)  65.7 us
    psum x1, blocking collectives, local(): lax.psum((grad_attention, grad_query, grad_key, grad_value, grad_output,...  39.6 us
    while x5, local copies, waits for them, and re-layouts, local(): lax.map(attend_forward, (query_all, key_all, value_all, valid))  35 us
    unnamed x132, local copies, waits for them, and re-layouts  34.2 us
    dot_general x4, matrix products, attend_backward(): jnp.einsum('ihd,jhd->hij', context_grad, value_rows, preferred_element_ty...  30 us
  transfers between devices with their start and end apart: 1, of which 1 were waited for; matrix products, arithmetic and copies ran while one was open for 7% of the time, Pallas kernels for 0%

commit v1 on v0

--- a/solution.py
+++ b/solution.py
@@ -108,7 +108,15 @@
     pooled = jnp.sum(final.reshape(seqs, slot_len, width) * pool_weight[:, :, None], axis=1)
     inverse_pool = lax.rsqrt(jnp.sum(pooled * pooled, axis=-1, keepdims=True) + epsilon)
     unit = pooled * inverse_pool
-    gathered = lax.all_gather(unit, ("tower", "batch"), axis=0, tiled=True)
+    ways, here = (lax.axis_size(("tower", "batch")), lax.axis_index(("tower", "batch")))
+    grown, reach = (unit, 1)
+    while reach < ways:
+        theirs = lax.ppermute(grown, ("tower", "batch"), [(d, d ^ reach) for d in range(ways)])
+        mine_first = jnp.concatenate([grown, theirs], axis=0)
+        theirs_first = jnp.concatenate([theirs, grown], axis=0)
+        grown = jnp.where(here & reach == 0, mine_first, theirs_first)
+        reach = 2 * reach
+    gathered = grown
     total_seqs = gathered.shape[0] // 2
     query_units = gathered[:total_seqs]
     doc_units = gathered[total_seqs:]

time: 1080 us -> 1040 us (0.963)
  blocking collectives: 112 us -> 42.3 us
  waiting for transfers between devices: 321 us -> 334 us
    all_gather x1 -> x0, blocking collectives: 72.1 us -> none  [local(): gathered = lax.all_gather(unit, ('tower', 'batch'), axis=0, tiled=True)]
    ppermute x0 -> x5, waiting for transfers between devices: none -> 10.8 us  [local(): lax.ppermute(grown, ('tower', 'batch'), [(d, d ^ reach) for d in range(wa...]
    unnamed x132 -> x140, local copies, waits for them, and re-layouts: 34.2 us -> 35.3 us
  transfers between devices with their start and end apart: 1 -> 6, of which waited for: 1 -> 6; matrix products, arithmetic and copies ran while one was open for 7% -> 7% of each run, Pallas kernels for 0% -> 0%
where the time goes in v1:
time: 1040 us; the launch traced here: 1030 us
  matrix products  366 us (35%)
  waiting for transfers between devices  334 us (32%)
  local copies, waits for them, and re-layouts  154 us (15%)
  other arithmetic  107 us (10%)
  blocking collectives  42.3 us (4%)
  between operations  18.1 us (2%)
  starting transfers between devices  10.8 us (1%)
    psum x1, waiting for transfers between devices, local(): lax.psum((grad_attention, grad_query, grad_key, grad_value, grad_output,...  323 us
    dot_general x8, matrix products, score_block(): jnp.einsum('ihd,jhd->hij', query_rows, key_rows, preferred_element_type=j...  67.1 us
    convert_element_type x4, other arithmetic, attend_backward(): scores_low = grad_scores.astype(jnp.bfloat16)  65.7 us
    psum x1, blocking collectives, local(): lax.psum((grad_attention, grad_query, grad_key, grad_value, grad_output,...  42.3 us
    while x5, local copies, waits for them, and re-layouts, local(): lax.map(attend_forward, (query_all, key_all, value_all, valid))  35.4 us
    unnamed x140, local copies, waits for them, and re-layouts  35.3 us
    dot_general x4, matrix products, attend_backward(): jnp.einsum('ihd,jhd->hij', context_grad, value_rows, preferred_element_ty...  30 us
    while x4, local copies, waits for them, and re-layouts, local(): lax.scan(attend_backward, jnp.zeros(bias.shape, jnp.float32), (query_all,...  27.5 us
  transfers between devices with their start and end apart: 6, of which 6 were waited for; matrix products, arithmetic and copies ran while one was open for 7% of the time, Pallas kernels for 0%

profile of v1, /device:TPU:0, one launch (start us, length us, event | category | flops | bytes accessed | tf_op | source)
XLA Modules:
  0.0 1032.5 jit_solution(5412967209169380705)
XLA Ops:
  74.4 13.6 %fusion.55 = f32[12,512,512]{2,0,1:T(8,128)} fusion(s32[512,512]{1,0:T(8,128)S(1)} %fusion.93, f32[32,12]{0,1:T(8,128)S(1)} %copy-done.38), kind=kOutput, calls=%fused_computation.65 | convolution fusion | flops 1216348160 | bytes 13633024 | tf_op jit(solution)/shard_map/ijb,bh->hij/dot_general | solution.py:65
  88.1 17.7 %copy.51 = f32[12,512,512]{1,2,0:T(8,128)} copy(f32[12,512,512]{2,0,1:T(8,128)} %fusion.55) | data formatting | bytes 25165824 | tf_op jit(solution)/shard_map/while | solution.py:97
  107.8 59.5 %while.29 = (s32[]{:T(128)}, bf16[4,512,12,64]{1,3,2,0:T(8,128)(2,1)}, f32[4,12,512]{2,1,0:T(8,128)}, bf16[4,512,12,64]{1,3,2,0:T(8,128)(2,1)}, pred[4,512]{1,0:...) while((s32[]{:T(128)}, ...), condition=%wide.region_4.5_spmd, body=%wide.region_1.4_spmd.sunk | while | flops 830859264 | bytes 53685868 | solution.py:97
  179.0 13.7 %fusion.117 = f32[2048,3072]{1,0:T(8,128)} fusion(bf16[768,3072]{1,0:T(8,128)(2,1)S(1)} %bitcast.266, f32[2048,768]{1,0:T(8,128)S(1)} %get-tuple-element.284, f32[768]{0:T(1024)S(1)} %copy-done.48, f32[2048]{0:T(1024)S(1)} %get-tuple-element.276), kind=kOutput, calls=%fused_computation.179 | convolution fusion | flops 9668395008 | bytes 36187136 | tf_op jit(solution)/shard_map/dot_general | solution.py:102
  192.8 18.1 %multiply_reduce_fusion.4 = (f32[2048]{0:T(1024)S(1)}, f32[2048,768]{1,0:T(8,128)}) fusion(f32[2048,768]{1,0:T(8,128)} %copy-done.16, bf16[3072,768]{1,0:T(8,128)(2,1)S(1)} %bitcast.264, f32[2048,3072]{1,0:T(8,128)} %fusion.117), kind=kOutput, calls=%fused_computation.101 | convolution fusion | flops 9687267328 | bytes 42475520 | tf_op jit(solution)/shard_map/dot_general | solution.py:104
  248.1 17.4 %fusion.83 = f32[3072,768]{1,0:T(8,128)} fusion(bf16[2048,768]{1,0:T(8,128)(2,1)S(1)} %fusion.82, f32[2048,3072]{1,0:T(8,128)} %fusion.117), kind=kOutput, calls=%fused_computation.110 | convolution fusion | flops 9682550784 | bytes 37748736 | tf_op jit(solution)/shard_map/tf,td->fd/dot_general | solution.py:152
  265.6 20.9 %fusion.52 = bf16[2048,3072]{1,0:T(8,128)(2,1)} fusion(f32[2048,3072]{1,0:T(8,128)} %fusion.117, bf16[2048,768]{1,0:T(8,128)(2,1)} %copy-done.22, bf16[3072,768]{1,0:T(8,128)(2,1)} %param.30), kind=kOutput, calls=%fused_computation.62 | convolution fusion | flops 9682550784 | bytes 45613056 | tf_op jit(solution)/shard_map/td,fd->tf/dot_general | solution.py:153
  286.5 19.3 %multiply_reduce_fusion.1 = (f32[768]{0:T(1024)}, f32[2048]{0:T(1024)S(1)}, f32[2048,768]{1,0:T(8,128)}) fusion(f32[2048,768]{1,0:T(8,128)} %copy-done.16, f32[2048]{0:T(1024)S(1)} %get-tuple-element.276, f32[768]{0:T(1024)S(1)} %copy-done.48, bf16[2048,3072]{1,0:T(8,128)(2,1)} %fusion.52, bf16[768,3072]{1,0:T(8,128)(2,1)} %param.29), kind=kOutput, calls=%fused_computation.95 | convolution fusion | flops 9673110528 | bytes 29906944 | tf_op jit(solution)/shard_map/tf,df->td/dot_general | solution.py:158
  305.8 15.6 %fusion.116 = f32[768,3072]{1,0:T(8,128)} fusion(bf16[2048,3072]{1,0:T(8,128)(2,1)} %fusion.52, f32[2048,768]{1,0:T(8,128)S(1)} %bitcast.248, f32[768]{0:T(1024)S(1)} %copy-done.48, f32[2048]{0:T(1024)S(1)} %get-tuple-element.276), kind=kOutput, calls=%fused_computation.178 | convolution fusion | flops 9668395008 | bytes 28322816 | tf_op jit(solution)/shard_map/td,tf->df/dot_general | solution.py:157
  354.8 183.0 %while.30 = (s32[]{:T(128)}, f32[12,512,512]{1,2,0:T(8,128)}, bf16[4,512,12,64]{1,3,2,0:T(8,128)(2,1)}, bf16[4,512,12,64]{1,3,2,0:T(8,128)(2,1)}, bf16[4,512,12,...) while((s32[]{:T(128)}, f32[12,512,512]{1,2,0:T(8,128)}, ...), condition=%wide.region_22.23_spmd.clone, body=%wide.region_20.22_spmd.clone.sunk | while | flops 2049042432 | bytes 177863392 | solution.py:202
  355.6 8.8 subtract_exponential_fusion.5
  374.8 13.5 %fusion.187 = (bf16[12,512,512]{1,2,0:T(8,128)(2,1)}, f32[12,512,512]{1,2,0:T(8,128)}) fusion(f32[12,512,512]{1,2,0:T(8,128)S(1)} %subtract_exponential_fusion.5, f32[12,512,512]{1,2,0:T(8,128)} %get-tuple-element.424, f32[12,512]{1,0:T(8,128)S(1)} %get-tuple-element.425, f32[12,512,512]{1,2,0:T(8,128)} %get-tuple-element.470, pred[]{:T(512)S(6)} %compare.3), kind=kLoop, calls=%fused_computation.24.clone.1 | loop fusion | flops 15728640 | bytes 56647680 | tf_op jit(solution)/shard_map/while/body/eval_jaxpr/convert_element_type | solution.py:186
  398.3 8.8 subtract_exponential_fusion.5
  417.5 17.4 %fusion.187 = (bf16[12,512,512]{1,2,0:T(8,128)(2,1)}, f32[12,512,512]{1,2,0:T(8,128)}) fusion(f32[12,512,512]{1,2,0:T(8,128)S(1)} %subtract_exponential_fusion.5, f32[12,512,512]{1,2,0:T(8,128)} %get-tuple-element.424, f32[12,512]{1,0:T(8,128)S(1)} %get-tuple-element.425, f32[12,512,512]{1,2,0:T(8,128)} %get-tuple-element.470, pred[]{:T(512)S(6)} %compare.3), kind=kLoop, calls=%fused_computation.24.clone.1 | loop fusion | flops 15728640 | bytes 56647680 | tf_op jit(solution)/shard_map/while/body/eval_jaxpr/convert_element_type | solution.py:186
  444.9 8.8 subtract_exponential_fusion.5
  464.2 17.4 %fusion.187 = (bf16[12,512,512]{1,2,0:T(8,128)(2,1)}, f32[12,512,512]{1,2,0:T(8,128)}) fusion(f32[12,512,512]{1,2,0:T(8,128)S(1)} %subtract_exponential_fusion.5, f32[12,512,512]{1,2,0:T(8,128)} %get-tuple-element.424, f32[12,512]{1,0:T(8,128)S(1)} %get-tuple-element.425, f32[12,512,512]{1,2,0:T(8,128)} %get-tuple-element.470, pred[]{:T(512)S(6)} %compare.3), kind=kLoop, calls=%fused_computation.24.clone.1 | loop fusion | flops 15728640 | bytes 56647680 | tf_op jit(solution)/shard_map/while/body/eval_jaxpr/convert_element_type | solution.py:186
  491.6 8.8 subtract_exponential_fusion.5
  510.9 17.4 %fusion.187 = (bf16[12,512,512]{1,2,0:T(8,128)(2,1)}, f32[12,512,512]{1,2,0:T(8,128)}) fusion(f32[12,512,512]{1,2,0:T(8,128)S(1)} %subtract_exponential_fusion.5, f32[12,512,512]{1,2,0:T(8,128)} %get-tuple-element.424, f32[12,512]{1,0:T(8,128)S(1)} %get-tuple-element.425, f32[12,512,512]{1,2,0:T(8,128)} %get-tuple-element.470, pred[]{:T(512)S(6)} %compare.3), kind=kLoop, calls=%fused_computation.24.clone.1 | loop fusion | flops 15728640 | bytes 56647680 | tf_op jit(solution)/shard_map/while/body/eval_jaxpr/convert_element_type | solution.py:186
  566.3 18.1 %copy.62 = f32[12,512,512]{2,0,1:T(8,128)} copy(f32[12,512,512]{1,2,0:T(8,128)} %get-tuple-element.126) | data formatting | bytes 25165824 | tf_op jit(solution)/shard_map/while | solution.py:202
  603.0 17.5 %fusion.92 = f32[32,12]{0,1:T(8,128)S(1)} fusion(f32[12,512,512]{2,0,1:T(8,128)S(1)} %copy-done.2, s32[512,512]{1,0:T(8,128)S(1)} %copy-done.11), kind=kOutput, calls=%fused_computation.121 | convolution fusion | flops 1216348160 | bytes 13633024 | tf_op jit(solution)/shard_map/ijb,hij->bh/dot_general | solution.py:210
  620.6 9.4 fusion.71
  630.0 42.3 %all-reduce = (f32[768]{0:T(1024)}, f32[32,12]{0,1:T(8,128)}, f32[768]{0:T(1024)}, f32[768]{0:T(1024)}) all-reduce(f32[768]{0:T(1024)S(1)} %get-tuple-element.208, f32[32,12]{0,1:T(8,128)S(1)} %fusion.92, f32[768]{0:T(1024)S(1)} %copy-done.49, f32[768]{0:T(1024)S(1)} %copy-done.35), channel_id=1, replica_groups=mesh['tower'=2,'batch'=16] {'tower','batch'}, use_global_device_ids=true, to_apply=%region_25.26 | all-reduce | flops 2688 | bytes 21504 | tf_op jit(solution)/shard_map/psum | solution.py:234
  680.6 323.0 %all-reduce.4.cloned.1.call-done = (f32[768,768]{1,0:T(8,128)}, f32[768,768]{1,0:T(8,128)}, f32[768,768]{1,0:T(8,128)}, f32[768,768]{1,0:T(8,128)}, f32[768,3072]{1,0:T(8,128)}, /*index=5*/f32[3072,768]{1,0:T(8,128)}) async-done(((f32[768,768]{1,0:T(8,128)}, f32[768,768]{1,0:T(8,128)}, f32[768,768]{1,0:T(8,128)}, f32[768,768]{1,0:T(8,128)}, f32[768,3072]{1,0:T(8,128)}, /*index=5*/f32[3072,768]{1,0:T(8,128)}), ...) | async-done | bytes 28311568 | tf_op jit(solution)/shard_map/psum | solution.py:234
  1011.3 9.3 copy.111
  (280 shorter events, 356.9 us)
Async XLA Ops:
  7.2 48.1 %copy-start = (bf16[768,768]{1,0:T(8,128)(2,1)S(1)}, bf16[768,768]{1,0:T(8,128)(2,1)}, u32[]{:S(2)}) copy-start(bf16[768,768]{1,0:T(8,128)(2,1)} %param.25) | copy-start | bytes 3538948
  7.2 996.5 %all-reduce.4.cloned.1.call-start = ((), (), s32[]{:S(2)}) async-start(), calls=%async_computation | async-start | bytes 56623104 | tf_op jit(solution)/shard_map/psum | solution.py:234
  7.7 66.8 %copy-start.10 = (s32[512,512]{1,0:T(8,128)}, s32[512,512]{1,0:T(8,128)S(1)}, u32[]{:S(2)}) copy-start(s32[512,512]{1,0:T(8,128)S(1)} %fusion.93) | copy-start | bytes 3145732
  12.5 42.8 %copy-start.29 = (f32[2048]{0:T(1024)}, f32[2048]{0:T(1024)S(1)}, u32[]{:S(2)}) copy-start(f32[2048]{0:T(1024)S(1)} %get-tuple-element.274) | copy-start | bytes 24580
  173.0 19.8 %slice-start.7 = ((s8[4718592]{0:T(1024)(128)(4,1)}), s8[4194304]{0:T(1024)(128)(4,1)S(1)}, s32[]{:S(2)}) async-start(s8[4718592]{0:T(1024)(128)(4,1)} %bitcast.263), calls=%async_computation.8 | async-start | bytes 8388608
  192.8 18.1 %copy-start.31 = (f32[768]{0:T(1024)S(1)}, f32[768]{0:T(1024)}, u32[]{:S(2)}) copy-start(f32[768]{0:T(1024)} %param.31) | copy-start | bytes 9220
  192.8 18.1 %copy-start.33 = (f32[4,512]{1,0:T(4,128)S(1)}, f32[4,512]{1,0:T(4,128)}, u32[]{:S(2)}) copy-start(f32[4,512]{1,0:T(4,128)} %get-tuple-element.280) | copy-start | bytes 24580
  210.9 24.9 %copy-start.34 = (f32[1,4,4,128]{3,2,1,0:T(4,128)S(1)}, f32[1,4,4,128]{3,2,1,0:T(4,128)}, u32[]{:S(2)}) copy-start(f32[1,4,4,128]{3,2,1,0:T(4,128)} %get-tuple-element.279) | copy-start | bytes 24580
  210.9 28.0 %copy-start.50 = (s32[64]{0:T(128)S(1)}, s32[64]{0:T(128)}, u32[]{:S(2)}) copy-start(s32[64]{0:T(128)} %param.21) | copy-start | bytes 772
  210.9 33.9 %slice-start = ((s8[6291456]{0:T(1024)(128)(4,1)}), s8[2097152]{0:T(1024)(128)(4,1)S(1)}, s32[]{:S(2)}) async-start(s8[6291456]{0:T(1024)(128)(4,1)} %bitcast.237), calls=%async_computation.1 | async-start | bytes 4194304
  214.6 4.6 collective-permute-start
  219.2 3.9 collective-permute-start.1
  223.2 4.1 collective-permute-start.2
  227.3 7.3 collective-permute-start.3
  235.7 1.6 collective-permute-start.4
  265.6 40.2 %slice-start.5 = ((s8[6291456]{0:T(1024)(128)(4,1)}), s8[2097152]{0:T(1024)(128)(4,1)S(1)}, s32[]{:S(2)}) async-start(s8[6291456]{0:T(1024)(128)(4,1)} %bitcast.247), calls=%async_computation.6 | async-start | bytes 4194304
  286.5 19.3 %slice-start.6 = ((s8[6291456]{0:T(1024)(128)(4,1)}), s8[4194304]{0:T(1024)(128)(4,1)S(1)}, s32[]{:S(2)}) async-start(s8[6291456]{0:T(1024)(128)(4,1)} %bitcast.247), calls=%async_computation.7 | async-start | bytes 8388608
  566.2 18.2 %copy-start.40 = (f32[64]{0:T(128)S(1)}, f32[64]{0:T(128)}, u32[]{:S(2)}) copy-start(f32[64]{0:T(128)} %copy-done.39) | copy-start | bytes 772
  566.2 18.1 %copy-start.42 = (f32[64]{0:T(128)S(1)}, f32[64]{0:T(128)}, u32[]{:S(2)}) copy-start(f32[64]{0:T(128)} %copy-done.41) | copy-start | bytes 772
  566.3 18.1 %copy-start.45 = (f32[64]{0:T(128)S(1)}, f32[64]{0:T(128)}, u32[]{:S(2)}) copy-start(f32[64]{0:T(128)} %copy-done.44) | copy-start | bytes 772
  566.3 18.1 %copy-start.47 = (f32[64]{0:T(128)S(1)}, f32[64]{0:T(128)}, u32[]{:S(2)}) copy-start(f32[64]{0:T(128)} %copy-done.46) | copy-start | bytes 772
  566.3 20.7 %copy-start.53 = (bf16[768,768]{1,0:T(8,128)(2,1)S(1)}, bf16[768,768]{1,0:T(8,128)(2,1)}, u32[]{:S(2)}) copy-start(bf16[768,768]{1,0:T(8,128)(2,1)} %param.23) | copy-start | bytes 3538948
  603.0 17.5 %copy-start.15 = (bf16[96,8,4,512]{3,1,2,0:T(8,128)(2,1)S(1)}, bf16[96,8,4,512]{3,1,2,0:T(8,128)(2,1)}, u32[]{:S(2)}) copy-start(bf16[96,8,4,512]{3,1,2,0:T(8,128)(2,1)} %copy-done.14) | copy-start | bytes 9437188
  620.6 51.7 %copy-start.32 = (f32[2048]{0:T(1024)S(1)}, f32[2048]{0:T(1024)}, u32[]{:S(2)}) copy-start(f32[2048]{0:T(1024)} %get-tuple-element.273) | copy-start | bytes 24580
  (54 other events, 375.5 us)
Sparse Core Ops, SparseCore 0:
  566.4 437.2 all-reduce.3
